TPU v7x, 32 devices: a whole 2x2x4 slice. The times are simulated.
32 devices in a mesh: seqa: 2 (over y), seqb: 4 (over z), tp: 4 (over x, core).
Axes of the slice: x: 2, y: 2, z: 4, core: 2. Of those that a mesh axis runs over, the one named last changes fastest.
Arguments:
- queries: bfloat16 [4096, 1024], P(('seqa', 'seqb'), 'tp'), may hold values from -6 to 6
- key_rows: bfloat16 [4096, 1024], P(('seqa', 'seqb'), 'tp'), may hold values from -6 to 6
- value_rows: bfloat16 [4096, 1024], P(('seqa', 'seqb'), 'tp'), may hold values from -6 to 6
- out_grad: bfloat16 [4096, 2048], P(('seqa', 'seqb'), 'tp'), may hold values from -6 to 6
- out_weight: bfloat16 [1024, 2048], P('tp'), may hold values from -0.1875 to 0.1875
- level_codes: int32 [4096, 160], P(('seqa', 'seqb'), 'tp'), may hold values from 0 to 7
Outputs:
- query_grad: bfloat16 [4096, 1024], P(('seqa', 'seqb'), 'tp')
- key_grad: bfloat16 [4096, 1024], P(('seqa', 'seqb'), 'tp')
- value_grad: bfloat16 [4096, 1024], P(('seqa', 'seqb'), 'tp')
All inputs are finite; a program needn't handle non-finite values.
Results may differ from a plain program's by a relative error of at most 0.0062.
Values may be sent and summed in bfloat16 or wider, within the bound.
A program may use at most 64 MiB of HBM per device.

v0:
```python
import math

import jax
import jax.numpy as jnp
from jax import lax
from jax.sharding import PartitionSpec as P

HEAD_DIM = 128


def swapped(x, axis, distance):
    return lax.ppermute(x, axis, [(i, i ^ 1 << distance) for i in range(lax.axis_size(axis))])


def per_device(queries, key_rows, value_rows, out_grad, out_weight, level_codes):
    shard_rows = queries.shape[0]
    head_count = out_weight.shape[0] // HEAD_DIM
    total_tokens = shard_rows * lax.axis_size(("seqa", "seqb"))
    scale_factor = 1.0 / math.sqrt(HEAD_DIM * total_tokens)
    head_grad = lax.dot_general(
        lax.all_gather(out_grad, "tp", axis=1, tiled=True),
        out_weight,
        (((1,), (1,)), ((), ())),
        preferred_element_type=jnp.float32,
    ).astype(jnp.bfloat16)
    level_weight = ((1 + level_codes).astype(jnp.float32) / 8.0).reshape(shard_rows, head_count, -1)
    shape_three = (shard_rows, head_count, HEAD_DIM)
    query_heads = queries.reshape(shape_three)
    key_head_matrix = key_rows.reshape(shape_three)
    value_head_matrix = value_rows.reshape(shape_three)
    grad_heads = head_grad.reshape(shape_three)
    level_top = shard_rows.bit_length() - 1
    span = min(shard_rows, 512)
    key_intra = jnp.zeros(shape_three, jnp.float32)
    value_intra = jnp.zeros(shape_three, jnp.float32)
    query_pos = jnp.arange(0, span, dtype=jnp.int32)[:, None]
    source_pos = jnp.arange(span, dtype=jnp.int32)[None, :]
    differ = jnp.bitwise_xor(query_pos, source_pos)
    level_map = jnp.zeros(differ.shape, jnp.int32)
    for bit_index in range(level_top):
        level_map = level_map + (differ >= 2**bit_index).astype(jnp.int32)
    causal = source_pos <= query_pos
    weight = jnp.zeros((head_count, span, span), jnp.float32)
    for level_index in range(level_top + 1):
        select = ((level_map == level_index) & causal).astype(jnp.float32)
        weight = weight + level_weight[:, :, level_index].T[:, :, None] * select[None]
    weight = weight * scale_factor
    scores = jnp.einsum(
        "thk,shk->hts", query_heads, key_head_matrix, preferred_element_type=jnp.float32
    )
    probs = (weight * scores).astype(jnp.bfloat16)
    dscore = jnp.einsum(
        "thv,shv->hts", grad_heads, value_head_matrix, preferred_element_type=jnp.float32
    )
    grad_mat = (weight * dscore).astype(jnp.bfloat16)
    query_parts = jnp.einsum(
        "hts,shk->thk", grad_mat, key_head_matrix, preferred_element_type=jnp.float32
    )
    key_intra = key_intra.at[:span].add(
        jnp.einsum("hts,thk->shk", grad_mat, query_heads, preferred_element_type=jnp.float32)
    )
    value_intra = value_intra.at[:span].add(
        jnp.einsum("hts,thv->shv", probs, grad_heads, preferred_element_type=jnp.float32)
    )
    carried_state = jnp.einsum(
        "ags,agr->gsr", key_head_matrix, value_head_matrix, preferred_element_type=jnp.float32
    )
    level_count = lax.axis_size(("seqa", "seqb")).bit_length() - 1
    device_index = lax.axis_index(("seqa", "seqb"))
    inter_weight = level_weight[:, :, level_top + 1 : level_top + 1 + level_count]
    scaled = (inter_weight[..., None] * grad_heads.astype(jnp.float32)[:, :, None, :]).astype(
        jnp.bfloat16
    )
    level_adjoint = scale_factor * jnp.einsum(
        "thk,thlv->lhkv", query_heads, scaled, preferred_element_type=jnp.float32
    )
    half_selector = [
        (device_index >> bit_index & 1).astype(jnp.float32) for bit_index in range(level_count)
    ]
    state_list = []
    total_adjoint = jnp.zeros(carried_state.shape, jnp.float32)
    for bit_index in range(level_count):
        upper = half_selector[bit_index]
        outgoing = upper * level_adjoint[bit_index] + (1.0 - upper) * carried_state
        received = swapped(outgoing, ("seqa", "seqb"), bit_index)
        for lower in range(bit_index):
            received = received + swapped(received, ("seqa", "seqb"), lower)
        state_list.append(received * upper)
        total_adjoint = total_adjoint + received * (1.0 - upper)
    level_states = jnp.stack(state_list, 0).astype(jnp.bfloat16)
    level_out = jnp.einsum(
        "thv,lhkv->thlk", grad_heads, level_states, preferred_element_type=jnp.float32
    )
    inter_sum = jnp.sum(inter_weight[..., None] * level_out, axis=2)
    adjoint_bfloat = total_adjoint.astype(jnp.bfloat16)
    query_grad = (query_parts + scale_factor * inter_sum).astype(jnp.bfloat16)
    key_grad = (
        key_intra
        + jnp.einsum(
            "ybe,bpe->ybp", value_head_matrix, adjoint_bfloat, preferred_element_type=jnp.float32
        )
    ).astype(jnp.bfloat16)
    value_grad = (
        value_intra
        + jnp.einsum(
            "mix,ixy->miy", key_head_matrix, adjoint_bfloat, preferred_element_type=jnp.float32
        )
    ).astype(jnp.bfloat16)
    flat = (shard_rows, head_count * HEAD_DIM)
    return (query_grad.reshape(flat), key_grad.reshape(flat), value_grad.reshape(flat))


def solution(mesh):
    placed = (
        P(("seqa", "seqb"), "tp"),
        P(("seqa", "seqb"), "tp"),
        P(("seqa", "seqb"), "tp"),
        P(("seqa", "seqb"), "tp"),
        P("tp", None),
        P(("seqa", "seqb"), "tp"),
    )
    return jax.shard_map(
        per_device,
        mesh=mesh,
        in_specs=placed,
        out_specs=(P(("seqa", "seqb"), "tp"), P(("seqa", "seqb"), "tp"), P(("seqa", "seqb"), "tp")),
        check_vma=False,
    )
```

profile of v0, /device:TPU:0, one launch (start us, length us, event | category | flops | bytes accessed | tf_op | source)
XLA Modules:
  0.0 76.9 jit_solution(2021714095588899248)
XLA Ops:
  7.9 0.9 %convert_multiply_fusion = f32[512,40]{0,1:T(8,128)S(1)} fusion(s32[512,40]{0,1:T(8,128)} %param.19), kind=kLoop, calls=%fused_computation.91 | loop fusion | flops 61440 | bytes 163840 | tf_op jit(solution)/shard_map/div | solution.py:26
  8.9 1.8 %fusion.35 = (f32[512,512]{1,0:T(8,128)}, f32[512,512]{1,0:T(8,128)}) fusion(), kind=kLoop, calls=%fused_computation.49 | loop fusion | flops 8912896 | bytes 2097152 | tf_op jit(solution)/shard_map/convert_element_type | solution.py:45
  10.6 1.9 %fusion.33 = (f32[512,512]{1,0:T(8,128)}, f32[512,512]{1,0:T(8,128)}) fusion(), kind=kLoop, calls=%fused_computation.47 | loop fusion | flops 8912896 | bytes 2097152 | tf_op jit(solution)/shard_map/convert_element_type | solution.py:45
  12.5 1.8 %fusion.31 = (f32[512,512]{1,0:T(8,128)}, f32[512,512]{1,0:T(8,128)}) fusion(), kind=kLoop, calls=%fused_computation.45 | loop fusion | flops 8912896 | bytes 2097152 | tf_op jit(solution)/shard_map/convert_element_type | solution.py:45
  14.4 1.8 %fusion.29 = (f32[512,512]{1,0:T(8,128)}, f32[512,512]{1,0:T(8,128)}) fusion(), kind=kLoop, calls=%fused_computation.43 | loop fusion | flops 8912896 | bytes 2097152 | tf_op jit(solution)/shard_map/convert_element_type | solution.py:45
  16.2 1.8 %fusion.27 = (f32[512,512]{1,0:T(8,128)}, f32[512,512]{1,0:T(8,128)}) fusion(), kind=kLoop, calls=%fused_computation.41 | loop fusion | flops 8912896 | bytes 2097152 | tf_op jit(solution)/shard_map/convert_element_type | solution.py:45
  18.0 16.8 %all-gather.2.cloned.1.call-done = bf16[512,2048]{1,0:T(8,128)(2,1)} async-done(((bf16[512,512]{1,0:T(8,128)(2,1)}), bf16[512,2048]{1,0:T(8,128)(2,1)}) %all-gather.2.cloned.1.call-update) | async-done | bytes 2097168 | tf_op jit(solution)/shard_map/all_gather | solution.py:21
  34.9 2.5 %convolution_convert_fusion = bf16[512,256]{0,1:T(8,128)(2,1)S(1)} fusion(bf16[512,2048]{1,0:T(8,128)(2,1)} %all-gather.2.cloned.1.call-done, bf16[256,2048]{1,0:T(8,128)(2,1)S(1)} %copy-done), kind=kOutput, calls=%fused_computation.15 | convolution fusion | flops 537001984 | bytes 3407872 | tf_op jit(solution)/shard_map/dot_general | solution.py:20
  37.9 0.9 %fusion.71 = (f32[2,128,128]{1,2,0:T(8,128)}, f32[2,128,128]{1,2,0:T(8,128)S(1)}, f32[2,128,128]{1,2,0:T(8,128)S(1)}) fusion(f32[3,2,128,128]{2,3,0,1:T(8,128)S(1)} %fusion.7, f32[]{:T(128)S(6)} %sub.12, f32[]{:T(128)S(6)} %convert_element_type.607, f32[]{:T(128)S(6)} %sub.14, f32[]{:T(128)S(6)} %convert_element_type.611, f32[]{:T(128)S(6)} %sub.13, ...), kind=kOutput, calls=%fused_computation.86 | convolution fusion | flops 33849344 | bytes 1310744 | tf_op jit(solution)/shard_map/ags,agr->gsr/dot_general | solution.py:65
  38.9 1.5 %collective-permute-start.3 = (f32[2,128,128]{1,2,0:T(8,128)S(1)}, f32[2,128,128]{1,2,0:T(8,128)S(1)}, u32[]{:S(2)}, u32[]{:S(2)}) collective-permute-start(f32[2,128,128]{1,2,0:T(8,128)S(1)} %get-tuple-element.50), channel_id=1, source_target_pairs={{0,16},{4,20},{8,24},{12,28},{16,0},{20,4},{24,8},{28,12},{1,17},{... | collective-permute-start | bytes 393224 | tf_op jit(solution)/shard_map/ppermute | solution.py:12
  40.4 3.5 %add_multiply_fusion = f32[2,512,512]{2,1,0:T(8,128)S(1)} fusion(f32[512,512]{1,0:T(8,128)S(1)} %copy-done.3, f32[2,512]{1,0:T(2,128)S(1)} %get-tuple-element.66, f32[512,512]{1,0:T(8,128)S(1)} %copy-done.2, f32[2,512]{1,0:T(2,128)S(1)} %get-tuple-element.67, f32[512,512]{1,0:T(8,128)S(1)} %copy-done.5, f32[2,512]{1,0:T(2,128)S(1)} %get-tuple-element.68, ...), kind=kLoop, calls=%fused_computation.2 | loop fusion | flops 10485760 | bytes 12623872 | tf_op jit(solution)/shard_map/mul | solution.py:47
  43.9 2.5 %collective-permute-start.1 = (f32[2,128,128]{1,2,0:T(8,128)S(1)}, f32[2,128,128]{1,2,0:T(8,128)}, u32[]{:S(2)}, u32[]{:S(2)}) collective-permute-start(f32[2,128,128]{1,2,0:T(8,128)S(1)} %get-tuple-element.51), channel_id=1, source_target_pairs={{0,8},{4,12},{8,0},{12,4},{16,24},{20,28},{24,16},{28,20},{1,9},{5... | collective-permute-start | bytes 393224 | tf_op jit(solution)/shard_map/ppermute | solution.py:12
  46.4 1.5 %collective-permute-start.4 = (f32[2,128,128]{1,2,0:T(8,128)S(1)}, f32[2,128,128]{1,2,0:T(8,128)S(1)}, u32[]{:S(2)}, u32[]{:S(2)}) collective-permute-start(f32[2,128,128]{1,2,0:T(8,128)S(1)} %collective-permute-done.3), channel_id=1, source_target_pairs={{0,4},{4,0},{8,12},{12,8},{16,20},{20,16},{24,28},{28,24},{1,5},{5... | collective-permute-start | bytes 393224 | tf_op jit(solution)/shard_map/ppermute | solution.py:12
  47.9 1.5 %multiply_convert_fusion.1 = bf16[2,512,512]{2,1,0:T(8,128)(2,1)} fusion(f32[2,512,512]{2,1,0:T(8,128)S(1)} %add_multiply_fusion, bf16[512,2,128]{0,2,1:T(8,128)(2,1)S(1)} %bitcast.185, bf16[512,256]{1,0:T(8,128)(2,1)S(1)} %copy-done.14), kind=kOutput, calls=%fused_computation.1 | convolution fusion | flops 135266304 | bytes 3670016 | tf_op jit(solution)/shard_map/thv,shv->hts/dot_general | solution.py:52
  49.9 3.4 %collective-permute-done.1 = f32[2,128,128]{1,2,0:T(8,128)} collective-permute-done((f32[2,128,128]{1,2,0:T(8,128)S(1)}, f32[2,128,128]{1,2,0:T(8,128)}, u32[]{:S(2)}, u32[]{:S(2)}) %collective-permute-start.1) | collective-permute-done | bytes 131104 | tf_op jit(solution)/shard_map/ppermute | solution.py:12
  53.8 3.4 %collective-permute-start.5 = (f32[2,128,128]{1,2,0:T(8,128)S(1)}, f32[2,128,128]{1,2,0:T(8,128)}, u32[]{:S(2)}, u32[]{:S(2)}) collective-permute-start(f32[2,128,128]{1,2,0:T(8,128)S(1)} %add.524), channel_id=1, source_target_pairs={{0,8},{4,12},{8,0},{12,4},{16,24},{20,28},{24,16},{28,20},{1,9},{5... | collective-permute-start | bytes 393224 | tf_op jit(solution)/shard_map/ppermute | solution.py:12
  57.2 2.4 %fusion.1 = f32[2,128,512]{2,1,0:T(8,128)} fusion(bf16[512,2,128]{0,2,1:T(8,128)(2,1)S(1)} %bitcast.186, f32[2,512,512]{2,1,0:T(8,128)S(1)} %add_multiply_fusion, bf16[512,256]{1,0:T(8,128)(2,1)} %param.14, bf16[512,256]{1,0:T(8,128)(2,1)} %param.15), kind=kOutput, calls=%fused_computation.6 | convolution fusion | flops 269484032 | bytes 3407872 | tf_op jit(solution)/shard_map/hts,thv->shv/dot_general | solution.py:63
  59.6 2.0 %collective-permute-done.2 = f32[2,128,128]{1,2,0:T(8,128)} collective-permute-done((f32[2,128,128]{1,2,0:T(8,128)}, f32[2,128,128]{1,2,0:T(8,128)}, u32[]{:S(2)}, u32[]{:S(2)}) %collective-permute-start.2) | collective-permute-done | bytes 131104 | tf_op jit(solution)/shard_map/ppermute | solution.py:12
  61.7 1.9 %collective-permute-done.5 = f32[2,128,128]{1,2,0:T(8,128)} collective-permute-done((f32[2,128,128]{1,2,0:T(8,128)S(1)}, f32[2,128,128]{1,2,0:T(8,128)}, u32[]{:S(2)}, u32[]{:S(2)}) %collective-permute-start.5) | collective-permute-done | bytes 131104 | tf_op jit(solution)/shard_map/ppermute | solution.py:12
  63.5 1.2 %add_convert_fusion = (bf16[2,128,128]{1,2,0:T(8,128)(2,1)S(1)}, bf16[1,2,128,128]{2,3,1,0:T(8,128)(2,1)S(1)}, bf16[1,2,128,128]{2,3,1,0:T(8,128)(2,1)S(1)}, bf16[1,2,128,128]{2,3,1,0:T(8,128)(2,1)S(1)}) fusion(f32[2,128,128]{1,2,0:T(8,128)} %collective-permute-done, f32[]{:T(128)S(6)} %sub.14, f32[]{:T(128)S(6)} %sub.13, f32[]{:T(128)S(6)} %sub.12, ...), kind=kLoop, calls=%fused_computation.87 | loop fusion | flops 458752 | bytes 917528 | tf_op jit(solution)/shard_map/convert_element_type | solution.py:95
  65.7 0.8 %copy.56 = bf16[512,256]{1,0:T(8,128)(2,1)} copy(bf16[512,256]{0,1:T(8,128)(2,1)S(1)} %bitcast.190) | data formatting | bytes 524288
  66.8 1.3 %fusion.5 = bf16[512,2,128]{0,2,1:T(8,128)(2,1)S(1)} fusion(f32[512,2,128]{0,2,1:T(8,128)S(1)} %convolution_bitcast_fusion.1, bf16[2,512,512]{2,1,0:T(8,128)(2,1)S(1)} %copy-done.1, bf16[512,256]{1,0:T(8,128)(2,1)} %param.14), kind=kOutput, calls=%fused_computation.14 | convolution fusion | flops 134479872 | bytes 2097152 | tf_op jit(solution)/shard_map/hts,thk->shk/dot_general | solution.py:60
  68.1 0.8 %copy.57 = bf16[512,256]{1,0:T(8,128)(2,1)} copy(bf16[512,256]{0,1:T(8,128)(2,1)S(1)} %bitcast.189) | data formatting | bytes 524288
  69.2 0.8 %copy.58 = bf16[512,256]{1,0:T(8,128)(2,1)} copy(bf16[512,256]{0,1:T(8,128)(2,1)S(1)} %bitcast.188) | data formatting | bytes 524288
  (58 shorter events, 3.8 us)
Async XLA Ops:
  7.2 27.7 %copy-start = (bf16[256,2048]{1,0:T(8,128)(2,1)S(1)}, bf16[256,2048]{1,0:T(8,128)(2,1)}, u32[]{:S(2)}) copy-start(bf16[256,2048]{1,0:T(8,128)(2,1)} %param.18) | copy-start | bytes 3145732
  7.2 27.7 %all-gather.2.cloned.1.call-start = ((), (), s32[]{:S(2)}) async-start(), calls=%async_computation | async-start | bytes 2621440 | tf_op jit(solution)/shard_map/all_gather | solution.py:21
  16.2 21.3 %copy-start.16 = (bf16[512,256]{1,0:T(8,128)(2,1)S(1)}, bf16[512,256]{1,0:T(8,128)(2,1)}, u32[]{:S(2)}) copy-start(bf16[512,256]{1,0:T(8,128)(2,1)} %param.14) | copy-start | bytes 786436
  16.2 21.7 %copy-start.13 = (bf16[512,256]{1,0:T(8,128)(2,1)S(1)}, bf16[512,256]{1,0:T(8,128)(2,1)}, u32[]{:S(2)}) copy-start(bf16[512,256]{1,0:T(8,128)(2,1)} %param.16) | copy-start | bytes 786436
  34.9 3.0 %copy-start.10 = (bf16[512,256]{1,0:T(8,128)(2,1)S(1)}, bf16[512,256]{1,0:T(8,128)(2,1)}, u32[]{:S(2)}) copy-start(bf16[512,256]{1,0:T(8,128)(2,1)} %param.15) | copy-start | bytes 786436
  34.9 5.5 %copy-start.5 = (f32[512,512]{1,0:T(8,128)S(1)}, f32[512,512]{1,0:T(8,128)}, u32[]{:S(2)}) copy-start(f32[512,512]{1,0:T(8,128)} %get-tuple-element.83) | copy-start | bytes 3145732
  34.9 5.5 %copy-start.6 = (f32[512,512]{1,0:T(8,128)S(1)}, f32[512,512]{1,0:T(8,128)}, u32[]{:S(2)}) copy-start(f32[512,512]{1,0:T(8,128)} %get-tuple-element.80) | copy-start | bytes 3145732
  34.9 5.5 %copy-start.7 = (f32[512,512]{1,0:T(8,128)S(1)}, f32[512,512]{1,0:T(8,128)}, u32[]{:S(2)}) copy-start(f32[512,512]{1,0:T(8,128)} %get-tuple-element.81) | copy-start | bytes 3145732
  34.9 5.4 %copy-start.8 = (f32[512,512]{1,0:T(8,128)S(1)}, f32[512,512]{1,0:T(8,128)}, u32[]{:S(2)}) copy-start(f32[512,512]{1,0:T(8,128)} %get-tuple-element.78) | copy-start | bytes 3145732
  34.9 5.4 %copy-start.9 = (f32[512,512]{1,0:T(8,128)S(1)}, f32[512,512]{1,0:T(8,128)}, u32[]{:S(2)}) copy-start(f32[512,512]{1,0:T(8,128)} %get-tuple-element.79) | copy-start | bytes 3145732
  37.4 2.9 %copy-start.2 = (f32[512,512]{1,0:T(8,128)S(1)}, f32[512,512]{1,0:T(8,128)}, u32[]{:S(2)}) copy-start(f32[512,512]{1,0:T(8,128)} %get-tuple-element.84) | copy-start | bytes 3145732
  37.4 2.9 %copy-start.3 = (f32[512,512]{1,0:T(8,128)S(1)}, f32[512,512]{1,0:T(8,128)}, u32[]{:S(2)}) copy-start(f32[512,512]{1,0:T(8,128)} %get-tuple-element.85) | copy-start | bytes 3145732
  37.4 2.9 %copy-start.4 = (f32[512,512]{1,0:T(8,128)S(1)}, f32[512,512]{1,0:T(8,128)}, u32[]{:S(2)}) copy-start(f32[512,512]{1,0:T(8,128)} %get-tuple-element.82) | copy-start | bytes 3145732
  38.9 7.5 %collective-permute-start.3 = (f32[2,128,128]{1,2,0:T(8,128)S(1)}, f32[2,128,128]{1,2,0:T(8,128)S(1)}, u32[]{:S(2)}, u32[]{:S(2)}) collective-permute-start(f32[2,128,128]{1,2,0:T(8,128)S(1)} %get-tuple-element.50), channel_id=1, source_target_pairs={{0,16},{4,20},{8,24},{12,28},{16,0},{20,4},{24,8},{28,12},{1,17},{... | collective-permute-start | bytes 393224 | tf_op jit(solution)/shard_map/ppermute | solution.py:12
  40.4 7.5 %copy-start.14 = (bf16[512,256]{1,0:T(8,128)(2,1)S(1)}, bf16[512,256]{1,0:T(8,128)(2,1)}, u32[]{:S(2)}) copy-start(bf16[512,256]{1,0:T(8,128)(2,1)} %param.16) | copy-start | bytes 786436
  43.9 9.3 %collective-permute-start.1 = (f32[2,128,128]{1,2,0:T(8,128)S(1)}, f32[2,128,128]{1,2,0:T(8,128)}, u32[]{:S(2)}, u32[]{:S(2)}) collective-permute-start(f32[2,128,128]{1,2,0:T(8,128)S(1)} %get-tuple-element.51), channel_id=1, source_target_pairs={{0,8},{4,12},{8,0},{12,4},{16,24},{20,28},{24,16},{28,20},{1,9},{5... | collective-permute-start | bytes 393224 | tf_op jit(solution)/shard_map/ppermute | solution.py:12
  46.4 7.4 %collective-permute-start.4 = (f32[2,128,128]{1,2,0:T(8,128)S(1)}, f32[2,128,128]{1,2,0:T(8,128)S(1)}, u32[]{:S(2)}, u32[]{:S(2)}) collective-permute-start(f32[2,128,128]{1,2,0:T(8,128)S(1)} %collective-permute-done.3), channel_id=1, source_target_pairs={{0,4},{4,0},{8,12},{12,8},{16,20},{20,16},{24,28},{28,24},{1,5},{5... | collective-permute-start | bytes 393224 | tf_op jit(solution)/shard_map/ppermute | solution.py:12
  49.4 10.3 %collective-permute-start = (f32[2,128,128]{1,2,0:T(8,128)}, f32[2,128,128]{1,2,0:T(8,128)}, u32[]{:S(2)}, u32[]{:S(2)}) collective-permute-start(f32[2,128,128]{1,2,0:T(8,128)} %get-tuple-element.49), channel_id=1, source_target_pairs={{0,4},{4,0},{8,12},{12,8},{16,20},{20,16},{24,28},{28,24},{1,5},{5... | collective-permute-start | bytes 393224 | tf_op jit(solution)/shard_map/ppermute | solution.py:12
  53.3 8.4 %collective-permute-start.2 = (f32[2,128,128]{1,2,0:T(8,128)}, f32[2,128,128]{1,2,0:T(8,128)}, u32[]{:S(2)}, u32[]{:S(2)}) collective-permute-start(f32[2,128,128]{1,2,0:T(8,128)} %collective-permute-done.1), channel_id=1, source_target_pairs={{0,4},{4,0},{8,12},{12,8},{16,20},{20,16},{24,28},{28,24},{1,5},{5... | collective-permute-start | bytes 393224 | tf_op jit(solution)/shard_map/ppermute | solution.py:12
  53.8 7.9 %copy-start.17 = (f32[2,128,128]{1,2,0:T(8,128)}, f32[2,128,128]{1,2,0:T(8,128)S(1)}, u32[]{:S(2)}) copy-start(f32[2,128,128]{1,2,0:T(8,128)S(1)} %add.524) | copy-start | bytes 393220
  53.8 9.7 %collective-permute-start.5 = (f32[2,128,128]{1,2,0:T(8,128)S(1)}, f32[2,128,128]{1,2,0:T(8,128)}, u32[]{:S(2)}, u32[]{:S(2)}) collective-permute-start(f32[2,128,128]{1,2,0:T(8,128)S(1)} %add.524), channel_id=1, source_target_pairs={{0,8},{4,12},{8,0},{12,4},{16,24},{20,28},{24,16},{28,20},{1,9},{5... | collective-permute-start | bytes 393224 | tf_op jit(solution)/shard_map/ppermute | solution.py:12
  59.6 5.6 %copy-start.1 = (bf16[2,512,512]{2,1,0:T(8,128)(2,1)S(1)}, bf16[2,512,512]{2,1,0:T(8,128)(2,1)}, u32[]{:S(2)}) copy-start(bf16[2,512,512]{2,1,0:T(8,128)(2,1)} %multiply_convert_fusion.1) | copy-start | bytes 3145732
  59.6 5.6 %copy-start.11 = (bf16[512,256]{1,0:T(8,128)(2,1)S(1)}, bf16[512,256]{1,0:T(8,128)(2,1)}, u32[]{:S(2)}) copy-start(bf16[512,256]{1,0:T(8,128)(2,1)} %param.15) | copy-start | bytes 786436
  65.7 3.3 %copy-start.12 = (f32[2,128,512]{2,1,0:T(8,128)S(1)}, f32[2,128,512]{2,1,0:T(8,128)}, u32[]{:S(2)}) copy-start(f32[2,128,512]{2,1,0:T(8,128)} %fusion.1) | copy-start | bytes 1572868
  (1 other events, 1.8 us)
Sparse Core Ops, SparseCore 0:
  9.5 25.2 all-gather.1
where the time goes:
time: 77.2 us; the launch traced here: 76.9 us
  waiting for transfers between devices  25 us (32%)
  other arithmetic  14.8 us (19%)
  between operations  14.4 us (19%)
  matrix products  10.4 us (13%)
  starting transfers between devices  9.74 us (13%)
  local copies, waits for them, and re-layouts  2.68 us (3%)
    all_gather x1, waiting for transfers between devices, per_device(): lax.all_gather(out_grad, 'tp', axis=1, tiled=True)  16.8 us
    ppermute x6, starting transfers between devices, swapped(): lax.ppermute(x, axis, [(i, i ^ 1 << distance) for i in range(lax.axis_siz...  9.7 us
    convert_element_type x5, other arithmetic, per_device(): select = ((level_map == level_index) & causal).astype(jnp.float32)  9.07 us
    ppermute x6, waiting for transfers between devices, swapped(): lax.ppermute(x, axis, [(i, i ^ 1 << distance) for i in range(lax.axis_siz...  7.45 us
    mul x1, other arithmetic, per_device(): weight = weight * scale_factor  3.52 us
    unnamed x39, local copies, waits for them, and re-layouts  2.61 us
    dot_general x1, matrix products, per_device(): lax.dot_general(lax.all_gather(out_grad, 'tp', axis=1, tiled=True), out_w...  2.49 us
    dot_general x1, matrix products, per_device(): jnp.einsum('hts,thv->shv', probs, grad_heads, preferred_element_type=jnp....  2.4 us
  transfers between devices with their start and end apart: 7, of which 5 were waited for; matrix products, arithmetic and copies ran while one was open for 23% of the time, Pallas kernels for 0%

commit v1 on v0

v1 whole, which is shorter than its diff:
```python
import functools
import math

import jax
import jax.numpy as jnp
from jax import lax
from jax.experimental import pallas as pl
from jax.experimental.pallas import tpu as pltpu
from jax.sharding import PartitionSpec as P

HEAD_DIM = 128
CHUNK = 128
MESH = pl.DeviceIdType.MESH
F32 = jnp.float32
BF16 = jnp.bfloat16


def dot(a, b, contract):
    return lax.dot_general(a, b, ((contract[:1], contract[1:]), ((), ())), preferred_element_type=F32)


def kernel(
    sizes,
    q_hbm, k_hbm, v_hbm, g_hbm, w_hbm, codes_hbm,
    qg_hbm, kg_hbm, vg_hbm,
    q_ref, k_ref, v_ref, codes_ref, lam_ref, gbuf, wbuf, hg_ref, probs_ref, gm_ref, diag_ref,
    qi_ref, ki_ref, vi_ref, la_ref, psum_ref, psend, precv, asend, arecv, out_ref,
    load_sem, wload_sem, gload_sem, store_sem,
    cross_send, cross_recv, fwd_send, fwd_recv, own_send, own_recv,
    state_send, state_recv, adj_send, adj_recv,
):
    seqa, seqb, tp, rows, heads, feat, scale = sizes
    chips = tp // 2
    chunks = rows // CHUNK
    levels = (seqa * seqb).bit_length() - 1
    top = rows.bit_length() - 1
    levmax = codes_hbm.shape[1] // heads
    ia, ib, it = lax.axis_index("seqa"), lax.axis_index("seqb"), lax.axis_index("tp")
    chip, core = it // 2, it % 2
    block = ia * seqb + ib

    def chip_at(offset):
        return lax.rem(chip + offset + chips, chips)

    partner = (ia, ib, chip * 2 + (1 - core))
    bit, mate = [], []
    for j in range(levels):
        value = (block // 2**j) % 2
        other = block + (1 - 2 * value) * 2**j
        bit.append(value)
        mate.append((other // seqb, other % seqb, it))
    crossing = [(ia, ib, chip_at(-k) * 2 + core) for k in range(chips)]

    barrier = pltpu.get_barrier_semaphore()
    peers = [partner] + crossing[1:] + mate
    for peer in peers:
        pl.semaphore_signal(barrier, inc=1, device_id=peer, device_id_type=MESH)

    loads = [
        pltpu.make_async_copy(src, dst, load_sem.at[i])
        for i, (src, dst) in enumerate(
            [(k_hbm, k_ref), (v_hbm, v_ref), (q_hbm, q_ref), (codes_hbm, codes_ref)]
        )
    ]
    for load in loads:
        load.start()
    gload = pltpu.make_async_copy(g_hbm, gbuf.at[0, 0], gload_sem)
    gload.start()
    wloads = []
    for k in range(chips):
        for cc in range(2):
            src = chip_at(k) * 2 + (core if cc == 0 else 1 - core)
            columns = pl.ds(pl.multiple_of(src * feat, feat), feat)
            copy = pltpu.make_async_copy(w_hbm.at[:, columns], wbuf.at[k, cc], wload_sem.at[k, cc])
            copy.start()
            wloads.append(copy)

    pl.semaphore_wait(barrier, len(peers))

    def rows_of(c):
        return pl.ds(c * CHUNK, CHUNK)

    def remote(src, dst, send, recv, device):
        return pltpu.make_async_remote_copy(
            src_ref=src, dst_ref=dst, send_sem=send, recv_sem=recv, device_id=device, device_id_type=MESH
        )

    cross = {}
    for c in range(chunks):
        for k in range(1, chips):
            cross[k, c] = remote(
                g_hbm.at[rows_of(c)], gbuf.at[k, 0, rows_of(c)],
                cross_send.at[k, c], cross_recv.at[k, c], crossing[k],
            )
            cross[k, c].start()
    own = remote(g_hbm, gbuf.at[0, 1], own_send, own_recv, partner)
    own.start()

    def cols(h):
        return slice(h * HEAD_DIM, (h + 1) * HEAD_DIM)

    loads[0].wait()
    loads[1].wait()
    state_copies = [
        remote(psend.at[j], precv.at[j], state_send.at[j], state_recv.at[j], mate[j]) for j in range(levels)
    ]
    for h in range(heads):
        state = dot(k_ref[:, cols(h)], v_ref[:, cols(h)], (0, 0))
        psum_ref[h] = state
        psend[0, h] = state.astype(BF16)
    state_copies[0].start()

    def state_step(j):
        state_copies[j].wait_recv()
        if j + 1 < levels:
            total = psum_ref[...] + precv[j].astype(F32)
            psum_ref[...] = total
            psend[j + 1] = total.astype(BF16)
            state_copies[j + 1].start()

    loads[2].wait()
    loads[3].wait()
    lam_ref[...] = (1 + codes_ref[...]).astype(F32) / 8.0

    def lam(c, h, level):
        at = h * levmax + level
        return lam_ref[c * CHUNK:(c + 1) * CHUNK, at:at + 1]

    row_at = lax.broadcasted_iota(jnp.int32, (CHUNK, CHUNK), 0)
    col_at = lax.broadcasted_iota(jnp.int32, (CHUNK, CHUNK), 1)
    differ = jnp.bitwise_xor(row_at, col_at)
    inner = CHUNK.bit_length() - 1
    causal = col_at <= row_at
    for h in range(heads):
        for c in range(chunks):
            weight = jnp.broadcast_to(lam(c, h, 0), (CHUNK, CHUNK))
            for level in range(1, inner + 1):
                weight = jnp.where(differ >= 2 ** (level - 1), lam(c, h, level), weight)
            diag_ref[h, c] = jnp.where(causal, weight, 0.0) * scale

    def weighted(c, h, values):
        pieces = []
        for s in range(c):
            factor = lam(c, h, inner + (c ^ s).bit_length()) * scale
            pieces.append((values[:, s * CHUNK:(s + 1) * CHUNK] * factor).astype(BF16))
        pieces.append((values[:, c * CHUNK:] * diag_ref[h, c]).astype(BF16))
        return pieces

    def attend(c, h, target, left_ref, right_ref):
        left = left_ref[c * CHUNK:(c + 1) * CHUNK, cols(h)]
        values = dot(left, right_ref[:(c + 1) * CHUNK, cols(h)], (1, 1))
        for s, piece in enumerate(weighted(c, h, values)):
            target[h, c * CHUNK:(c + 1) * CHUNK, s * CHUNK:(s + 1) * CHUNK] = piece

    for h in range(heads):
        for c in range(chunks):
            attend(c, h, probs_ref, q_ref, k_ref)

    gload.wait()
    for copy in wloads:
        copy.wait()

    def intra_rows(c):
        for h in range(heads):
            attend(c, h, gm_ref, hg_ref, v_ref)
            width = (c + 1) * CHUNK
            qi_ref[c * CHUNK:width, cols(h)] = dot(
                gm_ref[h, c * CHUNK:width, :width], k_ref[:width, cols(h)], (1, 0)
            )

    fwd = {}
    for c in range(chunks):
        here = slice(c * CHUNK, (c + 1) * CHUNK)
        partial = dot(gbuf[0, 0, here], wbuf[0, 0], (1, 1))
        if c == 0:
            own.wait_recv()
        partial = partial + dot(gbuf[0, 1, here], wbuf[0, 1], (1, 1))
        for k in range(1, chips):
            cross[k, c].wait_recv()
            fwd[k, c] = remote(
                gbuf.at[k, 0, rows_of(c)], gbuf.at[k, 1, rows_of(c)],
                fwd_send.at[k, c], fwd_recv.at[k, c], partner,
            )
            fwd[k, c].start()
            partial = partial + dot(gbuf[k, 0, here], wbuf[k, 0], (1, 1))
        for k in range(1, chips):
            fwd[k, c].wait_recv()
            partial = partial + dot(gbuf[k, 1, here], wbuf[k, 1], (1, 1))
        head_grad = partial.astype(BF16)
        hg_ref[here] = head_grad
        wide = head_grad.astype(F32)
        for h in range(heads):
            for i in range(levels):
                scaled = (lam(c, h, top + 1 + i) * wide[:, cols(h)]).astype(BF16)
                part = dot(q_ref[here, cols(h)], scaled, (0, 0)) * scale
                la_ref[i, h] = part if c == 0 else la_ref[i, h] + part
        if c < chunks - 1:
            intra_rows(c)
            if c < levels:
                state_step(c)

    adj = {
        (j, h): remote(asend.at[j, h], arecv.at[j, h], adj_send.at[j, h], adj_recv.at[j, h], mate[j])
        for j in range(levels)
        for h in range(heads)
    }
    for h in range(heads):
        asend[levels - 1, h] = jnp.where(bit[levels - 1] == 1, la_ref[levels - 1, h], 0.0).astype(BF16)
        adj[levels - 1, h].start()

    def tail_rows():
        intra_rows(chunks - 1)

    def tail_inter():
        for j in range(chunks - 1, levels):
            state_step(j)
        for h in range(heads):
            for c in range(chunks):
                here = slice(c * CHUNK, (c + 1) * CHUNK)
                total = jnp.zeros((CHUNK, HEAD_DIM), F32)
                for i in range(levels):
                    kept = jnp.where(bit[i] == 1, precv[i, h].astype(F32), 0.0).astype(BF16)
                    total = total + lam(c, h, top + 1 + i) * dot(hg_ref[here, cols(h)], kept, (1, 1))
                out_ref[0, here, cols(h)] = (qi_ref[here, cols(h)] + scale * total).astype(BF16)
        stores[0].start()

    def tail_columns():
        for h in range(heads):
            for s in range(chunks):
                start = s * CHUNK
                at = slice(start, start + CHUNK)
                ki_ref[at, cols(h)] = dot(gm_ref[h, start:, at], q_ref[start:, cols(h)], (0, 0))
                vi_ref[at, cols(h)] = dot(probs_ref[h, start:, at], hg_ref[start:, cols(h)], (0, 0))

    stores = [
        pltpu.make_async_copy(out_ref.at[i], ref, store_sem.at[i]) for i, ref in enumerate((qg_hbm, kg_hbm, vg_hbm))
    ]
    work = [tail_rows, tail_inter, tail_columns]
    total = [jnp.zeros((HEAD_DIM, HEAD_DIM), F32)] * heads
    for j in range(levels - 1, -1, -1):
        if work:
            work.pop(0)()
        for h in range(heads):
            adj[j, h].wait_recv()
            total[h] = total[h] + arecv[j, h].astype(F32)
            if j > 0:
                asend[j - 1, h] = (total[h] + jnp.where(bit[j - 1] == 1, la_ref[j - 1, h], 0.0)).astype(BF16)
                adj[j - 1, h].start()
    for piece in work:
        piece()
    for h in range(heads):
        adjoint = total[h].astype(BF16)
        out_ref[1, :, cols(h)] = (ki_ref[:, cols(h)] + dot(v_ref[:, cols(h)], adjoint, (1, 1))).astype(BF16)
        out_ref[2, :, cols(h)] = (vi_ref[:, cols(h)] + dot(k_ref[:, cols(h)], adjoint, (1, 0))).astype(BF16)
    stores[1].start()
    stores[2].start()
    for copy in cross.values():
        copy.wait_send()
    for copy in fwd.values():
        copy.wait_send()
    own.wait_send()
    for copy in state_copies:
        copy.wait_send()
    for copy in adj.values():
        copy.wait_send()
    for store in stores:
        store.wait()


def solution(mesh):
    seqa, seqb, tp = (mesh.shape[name] for name in ("seqa", "seqb", "tp"))
    levels = (seqa * seqb).bit_length() - 1

    def per_device(queries, key_rows, value_rows, out_grad, out_weight, level_codes):
        rows, width = queries.shape
        heads = width // HEAD_DIM
        feat = out_grad.shape[1]
        chips = tp // 2
        chunks = rows // CHUNK
        scale = 1.0 / math.sqrt(HEAD_DIM * rows * seqa * seqb)
        square = (HEAD_DIM, HEAD_DIM)
        dma = pltpu.SemaphoreType.DMA
        result = jax.ShapeDtypeStruct((rows, width), BF16)
        return pl.pallas_call(
            functools.partial(kernel, (seqa, seqb, tp, rows, heads, feat, scale)),
            out_shape=(result,) * 3,
            in_specs=[pl.BlockSpec(memory_space=pl.ANY)] * 6,
            out_specs=(pl.BlockSpec(memory_space=pl.ANY),) * 3,
            scratch_shapes=[
                pltpu.VMEM((rows, width), BF16),
                pltpu.VMEM((rows, width), BF16),
                pltpu.VMEM((rows, width), BF16),
                pltpu.VMEM(level_codes.shape, jnp.int32),
                pltpu.VMEM(level_codes.shape, F32),
                pltpu.VMEM((chips, 2, rows, feat), BF16),
                pltpu.VMEM((chips, 2, width, feat), BF16),
                pltpu.VMEM((rows, width), BF16),
                pltpu.VMEM((heads, rows, rows), BF16),
                pltpu.VMEM((heads, rows, rows), BF16),
                pltpu.VMEM((heads, chunks, CHUNK, CHUNK), F32),
                pltpu.VMEM((rows, width), F32),
                pltpu.VMEM((rows, width), F32),
                pltpu.VMEM((rows, width), F32),
                pltpu.VMEM((levels, heads) + square, F32),
                pltpu.VMEM((heads,) + square, F32),
                pltpu.VMEM((levels, heads) + square, BF16),
                pltpu.VMEM((levels, heads) + square, BF16),
                pltpu.VMEM((levels, heads) + square, BF16),
                pltpu.VMEM((levels, heads) + square, BF16),
                pltpu.VMEM((3, rows, width), BF16),
                dma((4,)),
                dma((chips, 2)),
                dma,
                dma((3,)),
                dma((chips, chunks)),
                dma((chips, chunks)),
                dma((chips, chunks)),
                dma((chips, chunks)),
                dma,
                dma,
                dma((levels,)),
                dma((levels,)),
                dma((levels, heads)),
                dma((levels, heads)),
            ],
            compiler_params=pltpu.CompilerParams(
                collective_id=0, has_side_effects=True, vmem_limit_bytes=40 * 1024 * 1024
            ),
        )(queries, key_rows, value_rows, out_grad, out_weight, level_codes)

    sharded = P(("seqa", "seqb"), "tp")
    return jax.shard_map(
        per_device,
        mesh=mesh,
        in_specs=(sharded,) * 4 + (P("tp", None), sharded),
        out_specs=(sharded,) * 3,
        check_vma=False,
    )
```

time: 77.2 us -> 41.2 us (0.53)
  Pallas kernels: 0 us -> 32.9 us
  waiting for transfers between devices: 25 us -> 0 us
  other arithmetic: 14.8 us -> 0 us
  between operations: 14.4 us -> 0.67 us
  matrix products: 10.4 us -> 0 us
  starting transfers between devices: 9.74 us -> 0 us
  local copies, waits for them, and re-layouts: 2.68 us -> 7.32 us
    pallas_call x0 -> x1, Pallas kernels: none -> 32.9 us  [per_device(): pl.pallas_call(functools.partial(kernel, (seqa, seqb, tp, rows, heads, fe...]
    all_gather x1 -> x0, waiting for transfers between devices: 16.8 us -> none  [per_device(): lax.all_gather(out_grad, 'tp', axis=1, tiled=True)]
    dot_general x10 -> x0, matrix products: 10.4 us -> none  [the longest x1 2.49 us: per_device(): lax.dot_general(lax.all_gather(out_grad, 'tp', axis=1, tiled=True), out_w...]
    convert_element_type x7 -> x0, other arithmetic: 10.4 us -> none  [the longest x5 9.07 us: per_device(): select = ((level_map == level_index) & causal).astype(jnp.float32)]
    ppermute x6 -> x0, starting transfers between devices: 9.7 us -> none  [swapped(): lax.ppermute(x, axis, [(i, i ^ 1 << distance) for i in range(lax.axis_siz...]
    ppermute x6 -> x0, waiting for transfers between devices: 7.45 us -> none  [swapped(): lax.ppermute(x, axis, [(i, i ^ 1 << distance) for i in range(lax.axis_siz...]
    unnamed x39 -> x14, local copies, waits for them, and re-layouts: 2.61 us -> 7.32 us
    mul x1 -> x0, other arithmetic: 3.52 us -> none  [per_device(): weight = weight * scale_factor]
  transfers between devices with their start and end apart: 7 -> 0, of which waited for: 5 -> 0; matrix products, arithmetic and copies ran while one was open for 23% -> 0% of each run, Pallas kernels for 0% -> 0%
where the time goes in v1:
time: 41.2 us; the launch traced here: 40.9 us
  Pallas kernels  32.9 us (80%)
  local copies, waits for them, and re-layouts  7.32 us (18%)
  between operations  0.67 us (2%)
    pallas_call x1, Pallas kernels, per_device(): pl.pallas_call(functools.partial(kernel, (seqa, seqb, tp, rows, heads, fe...  32.9 us
    unnamed x14, local copies, waits for them, and re-layouts  7.32 us

profile of v1, /device:TPU:0, one launch (start us, length us, event | category | flops | bytes accessed | tf_op | source)
XLA Modules:
  0.0 40.9 jit_solution(17489757414402911462)
XLA Ops:
  0.6 0.0 copy-start.2
  0.6 1.1 %copy.9.codes_hbm = s32[512,40]{1,0:T(8,128)S(1)} copy(s32[512,40]{0,1:T(8,128)} %param.11) | data formatting | bytes 163840 | tf_op args[5]
  1.7 0.0 copy-done.2
  1.7 0.0 copy-start
  1.7 1.2 %copy-done = bf16[256,2048]{1,0:T(8,128)(2,1)S(1)} copy-done((bf16[256,2048]{1,0:T(8,128)(2,1)S(1)}, bf16[256,2048]{1,0:T(8,128)(2,1)}, u32[]{:S(2)}) %copy-start) | copy-done | bytes 1048600
  2.9 0.0 copy-start.1
  2.9 1.0 %copy-done.1 = bf16[512,512]{1,0:T(8,128)(2,1)S(1)} copy-done((bf16[512,512]{1,0:T(8,128)(2,1)S(1)}, bf16[512,512]{1,0:T(8,128)(2,1)}, u32[]{:S(2)}) %copy-start.1) | copy-done | bytes 524312
  4.0 0.0 copy-start.3
  4.0 0.9 %copy-done.3 = bf16[512,256]{1,0:T(8,128)(2,1)S(1)} copy-done((bf16[512,256]{1,0:T(8,128)(2,1)S(1)}, bf16[512,256]{1,0:T(8,128)(2,1)}, u32[]{:S(2)}) %copy-start.3) | copy-done | bytes 262168
  4.9 0.0 copy-start.4
  4.9 0.9 %copy-done.4 = bf16[512,256]{1,0:T(8,128)(2,1)S(1)} copy-done((bf16[512,256]{1,0:T(8,128)(2,1)S(1)}, bf16[512,256]{1,0:T(8,128)(2,1)}, u32[]{:S(2)}) %copy-start.4) | copy-done | bytes 262168
  5.9 32.9 %shard_map.85 = (bf16[512,256]{1,0:T(8,128)(2,1)S(1)}, bf16[512,256]{1,0:T(8,128)(2,1)S(1)}, bf16[512,256]{1,0:T(8,128)(2,1)S(1)}) custom-call(bf16[512,256]{1,0:T(8,128)(2,1)S(1)} %copy-done.2, bf16[512,256]{1,0:T(8,128)(2,1)S(1)} %copy-done.3, bf16[512,256]{1,0:T(8,128)(2,1)S(1)} %copy-done.4, bf16[512,512]{1,0:T(8,128)(2,1)S(1)} %copy-done.1, ...), custom_call_target="tpu_custom_call" | custom-call | tf_op jit(solution)/shard_map/pallas_call | solution.py:284
  38.8 0.7 %copy.13 = bf16[512,256]{1,0:T(8,128)(2,1)} copy(bf16[512,256]{1,0:T(8,128)(2,1)S(1)} %get-tuple-element.6) | data formatting | bytes 524288
  39.5 0.7 %copy.14 = bf16[512,256]{1,0:T(8,128)(2,1)} copy(bf16[512,256]{1,0:T(8,128)(2,1)S(1)} %get-tuple-element.7) | data formatting | bytes 524288
  40.2 0.7 %copy.15 = bf16[512,256]{1,0:T(8,128)(2,1)} copy(bf16[512,256]{1,0:T(8,128)(2,1)S(1)} %get-tuple-element.8) | data formatting | bytes 524288
Async XLA Ops:
  0.6 1.1 %copy-start.2 = (bf16[512,256]{1,0:T(8,128)(2,1)S(1)}, bf16[512,256]{1,0:T(8,128)(2,1)}, u32[]{:S(2)}) copy-start(bf16[512,256]{1,0:T(8,128)(2,1)} %q_hbm.1) | copy-start | bytes 786436
  1.7 1.2 %copy-start = (bf16[256,2048]{1,0:T(8,128)(2,1)S(1)}, bf16[256,2048]{1,0:T(8,128)(2,1)}, u32[]{:S(2)}) copy-start(bf16[256,2048]{1,0:T(8,128)(2,1)} %w_hbm.1) | copy-start | bytes 3145732
  2.9 1.0 %copy-start.1 = (bf16[512,512]{1,0:T(8,128)(2,1)S(1)}, bf16[512,512]{1,0:T(8,128)(2,1)}, u32[]{:S(2)}) copy-start(bf16[512,512]{1,0:T(8,128)(2,1)} %g_hbm.1) | copy-start | bytes 1572868
  4.0 0.9 %copy-start.3 = (bf16[512,256]{1,0:T(8,128)(2,1)S(1)}, bf16[512,256]{1,0:T(8,128)(2,1)}, u32[]{:S(2)}) copy-start(bf16[512,256]{1,0:T(8,128)(2,1)} %k_hbm.1) | copy-start | bytes 786436
  4.9 0.9 %copy-start.4 = (bf16[512,256]{1,0:T(8,128)(2,1)S(1)}, bf16[512,256]{1,0:T(8,128)(2,1)}, u32[]{:S(2)}) copy-start(bf16[512,256]{1,0:T(8,128)(2,1)} %v_hbm.1) | copy-start | bytes 786436

commit v2 on v1

--- a/solution.py
+++ b/solution.py
@@ -10,6 +10,7 @@
 
 HEAD_DIM = 128
 CHUNK = 128
+PIECES = 2
 MESH = pl.DeviceIdType.MESH
 F32 = jnp.float32
 BF16 = jnp.bfloat16
@@ -22,10 +23,10 @@
 def kernel(
     sizes,
     q_hbm, k_hbm, v_hbm, g_hbm, w_hbm, codes_hbm,
-    qg_hbm, kg_hbm, vg_hbm,
+    qg_ref, kg_ref, vg_ref,
     q_ref, k_ref, v_ref, codes_ref, lam_ref, gbuf, wbuf, hg_ref, probs_ref, gm_ref, diag_ref,
-    qi_ref, ki_ref, vi_ref, la_ref, psum_ref, psend, precv, asend, arecv, out_ref,
-    load_sem, wload_sem, gload_sem, store_sem,
+    qi_ref, ki_ref, vi_ref, la_ref, psum_ref, asum_ref, psend, precv, asend, arecv,
+    load_sem, wload_sem, gload_sem,
     cross_send, cross_recv, fwd_send, fwd_recv, own_send, own_recv,
     state_send, state_recv, adj_send, adj_recv,
 ):
@@ -34,7 +35,7 @@
     chunks = rows // CHUNK
     levels = (seqa * seqb).bit_length() - 1
     top = rows.bit_length() - 1
-    levmax = codes_hbm.shape[1] // heads
+    levmax = codes_hbm.shape[0] // heads
     ia, ib, it = lax.axis_index("seqa"), lax.axis_index("seqb"), lax.axis_index("tp")
     chip, core = it // 2, it % 2
     block = ia * seqb + ib
@@ -120,7 +121,7 @@
 
     loads[2].wait()
     loads[3].wait()
-    lam_ref[...] = (1 + codes_ref[...]).astype(F32) / 8.0
+    lam_ref[...] = ((1 + codes_ref[...]).astype(F32) / 8.0).T
 
     def lam(c, h, level):
         at = h * levmax + level
@@ -167,6 +168,23 @@
             qi_ref[c * CHUNK:width, cols(h)] = dot(
                 gm_ref[h, c * CHUNK:width, :width], k_ref[:width, cols(h)], (1, 0)
             )
+
+    step_rows = HEAD_DIM // PIECES
+    adj = {}
+    for j in range(levels):
+        for h in range(heads):
+            for p in range(PIECES):
+                at = pl.ds(p * step_rows, step_rows)
+                adj[j, h, p] = remote(
+                    asend.at[j, h, at], arecv.at[j, h, at],
+                    adj_send.at[j, h, p], adj_recv.at[j, h, p], mate[j],
+                )
+
+    def send_adjoint(j, h, value):
+        for p in range(PIECES):
+            at = slice(p * step_rows, (p + 1) * step_rows)
+            asend[j, h, at] = value[at].astype(BF16)
+            adj[j, h, p].start()
 
     fwd = {}
     for c in range(chunks):
@@ -189,24 +207,18 @@
         head_grad = partial.astype(BF16)
         hg_ref[here] = head_grad
         wide = head_grad.astype(F32)
-        for h in range(heads):
-            for i in range(levels):
+        for i in range(levels - 1, -1, -1):
+            for h in range(heads):
                 scaled = (lam(c, h, top + 1 + i) * wide[:, cols(h)]).astype(BF16)
                 part = dot(q_ref[here, cols(h)], scaled, (0, 0)) * scale
-                la_ref[i, h] = part if c == 0 else la_ref[i, h] + part
+                part = part if c == 0 else la_ref[i, h] + part
+                la_ref[i, h] = part
+                if c == chunks - 1 and i == levels - 1:
+                    send_adjoint(i, h, jnp.where(bit[i] == 1, part, 0.0))
         if c < chunks - 1:
             intra_rows(c)
             if c < levels:
                 state_step(c)
-
-    adj = {
-        (j, h): remote(asend.at[j, h], arecv.at[j, h], adj_send.at[j, h], adj_recv.at[j, h], mate[j])
-        for j in range(levels)
-        for h in range(heads)
-    }
-    for h in range(heads):
-        asend[levels - 1, h] = jnp.where(bit[levels - 1] == 1, la_ref[levels - 1, h], 0.0).astype(BF16)
-        adj[levels - 1, h].start()
 
     def tail_rows():
         intra_rows(chunks - 1)
@@ -221,8 +233,7 @@
                 for i in range(levels):
                     kept = jnp.where(bit[i] == 1, precv[i, h].astype(F32), 0.0).astype(BF16)
                     total = total + lam(c, h, top + 1 + i) * dot(hg_ref[here, cols(h)], kept, (1, 1))
-                out_ref[0, here, cols(h)] = (qi_ref[here, cols(h)] + scale * total).astype(BF16)
-        stores[0].start()
+                qg_ref[here, cols(h)] = (qi_ref[here, cols(h)] + scale * total).astype(BF16)
 
     def tail_columns():
         for h in range(heads):
@@ -232,28 +243,28 @@
                 ki_ref[at, cols(h)] = dot(gm_ref[h, start:, at], q_ref[start:, cols(h)], (0, 0))
                 vi_ref[at, cols(h)] = dot(probs_ref[h, start:, at], hg_ref[start:, cols(h)], (0, 0))
 
-    stores = [
-        pltpu.make_async_copy(out_ref.at[i], ref, store_sem.at[i]) for i, ref in enumerate((qg_hbm, kg_hbm, vg_hbm))
-    ]
     work = [tail_rows, tail_inter, tail_columns]
-    total = [jnp.zeros((HEAD_DIM, HEAD_DIM), F32)] * heads
     for j in range(levels - 1, -1, -1):
         if work:
             work.pop(0)()
         for h in range(heads):
-            adj[j, h].wait_recv()
-            total[h] = total[h] + arecv[j, h].astype(F32)
-            if j > 0:
-                asend[j - 1, h] = (total[h] + jnp.where(bit[j - 1] == 1, la_ref[j - 1, h], 0.0)).astype(BF16)
-                adj[j - 1, h].start()
+            for p in range(PIECES):
+                at = slice(p * step_rows, (p + 1) * step_rows)
+                adj[j, h, p].wait_recv()
+                total = arecv[j, h, at].astype(F32)
+                if j < levels - 1:
+                    total = asum_ref[h, at] + total
+                asum_ref[h, at] = total
+                if j > 0:
+                    addend = jnp.where(bit[j - 1] == 1, la_ref[j - 1, h, at], 0.0)
+                    asend[j - 1, h, at] = (total + addend).astype(BF16)
+                    adj[j - 1, h, p].start()
     for piece in work:
         piece()
     for h in range(heads):
-        adjoint = total[h].astype(BF16)
-        out_ref[1, :, cols(h)] = (ki_ref[:, cols(h)] + dot(v_ref[:, cols(h)], adjoint, (1, 1))).astype(BF16)
-        out_ref[2, :, cols(h)] = (vi_ref[:, cols(h)] + dot(k_ref[:, cols(h)], adjoint, (1, 0))).astype(BF16)
-    stores[1].start()
-    stores[2].start()
+        adjoint = asum_ref[h].astype(BF16)
+        kg_ref[:, cols(h)] = (ki_ref[:, cols(h)] + dot(v_ref[:, cols(h)], adjoint, (1, 1))).astype(BF16)
+        vg_ref[:, cols(h)] = (vi_ref[:, cols(h)] + dot(k_ref[:, cols(h)], adjoint, (1, 0))).astype(BF16)
     for copy in cross.values():
         copy.wait_send()
     for copy in fwd.values():
@@ -263,8 +274,15 @@
         copy.wait_send()
     for copy in adj.values():
         copy.wait_send()
-    for store in stores:
-        store.wait()
+
+
+def place(*refs):
+    sems = refs[6]
+    copies = [pltpu.make_async_copy(refs[i], refs[3 + i], sems.at[i]) for i in range(3)]
+    for copy in copies:
+        copy.start()
+    for copy in copies:
+        copy.wait()
 
 
 def solution(mesh):
@@ -281,16 +299,16 @@
         square = (HEAD_DIM, HEAD_DIM)
         dma = pltpu.SemaphoreType.DMA
         result = jax.ShapeDtypeStruct((rows, width), BF16)
-        return pl.pallas_call(
+        grads = pl.pallas_call(
             functools.partial(kernel, (seqa, seqb, tp, rows, heads, feat, scale)),
             out_shape=(result,) * 3,
-            in_specs=[pl.BlockSpec(memory_space=pl.ANY)] * 6,
-            out_specs=(pl.BlockSpec(memory_space=pl.ANY),) * 3,
+            in_specs=[pl.BlockSpec(memory_space=pltpu.HBM)] * 6,
+            out_specs=(pl.BlockSpec(memory_space=pltpu.VMEM),) * 3,
             scratch_shapes=[
                 pltpu.VMEM((rows, width), BF16),
                 pltpu.VMEM((rows, width), BF16),
                 pltpu.VMEM((rows, width), BF16),
-                pltpu.VMEM(level_codes.shape, jnp.int32),
+                pltpu.VMEM(level_codes.shape[::-1], jnp.int32),
                 pltpu.VMEM(level_codes.shape, F32),
                 pltpu.VMEM((chips, 2, rows, feat), BF16),
                 pltpu.VMEM((chips, 2, width, feat), BF16),
@@ -303,15 +321,14 @@
                 pltpu.VMEM((rows, width), F32),
                 pltpu.VMEM((levels, heads) + square, F32),
                 pltpu.VMEM((heads,) + square, F32),
+                pltpu.VMEM((heads,) + square, F32),
                 pltpu.VMEM((levels, heads) + square, BF16),
                 pltpu.VMEM((levels, heads) + square, BF16),
                 pltpu.VMEM((levels, heads) + square, BF16),
                 pltpu.VMEM((levels, heads) + square, BF16),
-                pltpu.VMEM((3, rows, width), BF16),
                 dma((4,)),
                 dma((chips, 2)),
                 dma,
-                dma((3,)),
                 dma((chips, chunks)),
                 dma((chips, chunks)),
                 dma((chips, chunks)),
@@ -320,13 +337,21 @@
                 dma,
                 dma((levels,)),
                 dma((levels,)),
-                dma((levels, heads)),
-                dma((levels, heads)),
+                dma((levels, heads, PIECES)),
+                dma((levels, heads, PIECES)),
             ],
             compiler_params=pltpu.CompilerParams(
-                collective_id=0, has_side_effects=True, vmem_limit_bytes=40 * 1024 * 1024
+                collective_id=0, has_side_effects=True, vmem_limit_bytes=32768 * 1024
             ),
-        )(queries, key_rows, value_rows, out_grad, out_weight, level_codes)
+        )(*[pltpu.with_memory_space_constraint(x, pltpu.HBM) for x in (queries, key_rows, value_rows, out_grad, out_weight, level_codes.T)])
+        return pl.pallas_call(
+            place,
+            out_shape=(result,) * 3,
+            in_specs=[pl.BlockSpec(memory_space=pltpu.VMEM)] * 3,
+            out_specs=(pl.BlockSpec(memory_space=pl.ANY),) * 3,
+            scratch_shapes=[dma((3,))],
+            compiler_params=pltpu.CompilerParams(vmem_limit_bytes=8 * 1024 * 1024),
+        )(*grads)
 
     sharded = P(("seqa", "seqb"), "tp")
     return jax.shard_map(

time: 41.2 us -> 34.6 us (0.84)
  local copies, waits for them, and re-layouts: 7.32 us -> 0 us
  Pallas kernels: 32.9 us -> 33.8 us
    unnamed x14 -> x0, local copies, waits for them, and re-layouts: 7.32 us -> none
    pallas_call x0 -> x1, Pallas kernels: none -> 0.9 us  [per_device(): pl.pallas_call(place, out_shape=(result,) * 3, in_specs=[pl.BlockSpec(mem...]
where the time goes in v2:
time: 34.6 us; the launch traced here: 34.4 us
  Pallas kernels  33.8 us (98%)
  between operations  0.64 us (2%)
    pallas_call x1, Pallas kernels, per_device(): pl.pallas_call(functools.partial(kernel, (seqa, seqb, tp, rows, heads, fe...  32.9 us
    pallas_call x1, Pallas kernels, per_device(): pl.pallas_call(place, out_shape=(result,) * 3, in_specs=[pl.BlockSpec(mem...  0.9 us

profile of v2, /device:TPU:0, one launch (start us, length us, event | category | flops | bytes accessed | tf_op | source)
XLA Modules:
  0.0 34.4 jit_solution(13278791305345486668)
XLA Ops:
  0.6 32.9 %shard_map.85 = (bf16[512,256]{1,0:T(8,128)(2,1)S(1)}, bf16[512,256]{1,0:T(8,128)(2,1)S(1)}, bf16[512,256]{1,0:T(8,128)(2,1)S(1)}) custom-call(bf16[512,256]{1,0:T(8,128)(2,1)} %q_hbm.1, bf16[512,256]{1,0:T(8,128)(2,1)} %k_hbm.1, bf16[512,256]{1,0:T(8,128)(2,1)} %v_hbm.1, bf16[512,512]{1,0:T(8,128)(2,1)} %g_hbm.1, bf16[256,2048]{1,0:T(8,128)(2,1)} %w_hbm.1, ...), custom_call_target="tpu_custom_call" | custom-call | tf_op jit(solution)/shard_map/pallas_call | solution.py:302
  33.5 0.9 %shard_map.86 = (bf16[512,256]{1,0:T(8,128)(2,1)}, bf16[512,256]{1,0:T(8,128)(2,1)}, bf16[512,256]{1,0:T(8,128)(2,1)}) custom-call(bf16[512,256]{1,0:T(8,128)(2,1)S(1)} %get-tuple-element.6.refs_0_, bf16[512,256]{1,0:T(8,128)(2,1)S(1)} %get-tuple-element.7.refs_1_, bf16[512,256]{1,0:T(8,128)(2,1)S(1)} %get-tuple-element.8.refs_2_), custom_call_target="tpu_custom_call" | custom-call | tf_op jit(solution)/shard_map/pallas_call | solution.py:347

commit v3 on v2

--- a/solution.py
+++ b/solution.py
@@ -186,6 +186,7 @@
             asend[j, h, at] = value[at].astype(BF16)
             adj[j, h, p].start()
 
+    state_step(0)
     fwd = {}
     for c in range(chunks):
         here = slice(c * CHUNK, (c + 1) * CHUNK)
@@ -217,14 +218,14 @@
                     send_adjoint(i, h, jnp.where(bit[i] == 1, part, 0.0))
         if c < chunks - 1:
             intra_rows(c)
-            if c < levels:
-                state_step(c)
+            if c + 1 < levels:
+                state_step(c + 1)
 
     def tail_rows():
         intra_rows(chunks - 1)
 
     def tail_inter():
-        for j in range(chunks - 1, levels):
+        for j in range(chunks, levels):
             state_step(j)
         for h in range(heads):
             for c in range(chunks):

time: 34.6 us -> 31.8 us (0.919)
  Pallas kernels: 33.8 us -> 31 us
    pallas_call x1, Pallas kernels: 32.9 us -> 30.1 us  [per_device(): pl.pallas_call(functools.partial(kernel, (seqa, seqb, tp, rows, heads, fe...]
where the time goes in v3:
time: 31.8 us; the launch traced here: 31.6 us
  Pallas kernels  31 us (97%)
  between operations  0.64 us (2%)
    pallas_call x1, Pallas kernels, per_device(): pl.pallas_call(functools.partial(kernel, (seqa, seqb, tp, rows, heads, fe...  30.1 us
    pallas_call x1, Pallas kernels, per_device(): pl.pallas_call(place, out_shape=(result,) * 3, in_specs=[pl.BlockSpec(mem...  0.9 us

profile of v3, /device:TPU:0, one launch (start us, length us, event | category | flops | bytes accessed | tf_op | source)
XLA Modules:
  0.0 31.6 jit_solution(16371743774202894637)
XLA Ops:
  0.6 30.1 %shard_map.85 = (bf16[512,256]{1,0:T(8,128)(2,1)S(1)}, bf16[512,256]{1,0:T(8,128)(2,1)S(1)}, bf16[512,256]{1,0:T(8,128)(2,1)S(1)}) custom-call(bf16[512,256]{1,0:T(8,128)(2,1)} %q_hbm.1, bf16[512,256]{1,0:T(8,128)(2,1)} %k_hbm.1, bf16[512,256]{1,0:T(8,128)(2,1)} %v_hbm.1, bf16[512,512]{1,0:T(8,128)(2,1)} %g_hbm.1, bf16[256,2048]{1,0:T(8,128)(2,1)} %w_hbm.1, ...), custom_call_target="tpu_custom_call" | custom-call | tf_op jit(solution)/shard_map/pallas_call | solution.py:303
  30.7 0.9 %shard_map.86 = (bf16[512,256]{1,0:T(8,128)(2,1)}, bf16[512,256]{1,0:T(8,128)(2,1)}, bf16[512,256]{1,0:T(8,128)(2,1)}) custom-call(bf16[512,256]{1,0:T(8,128)(2,1)S(1)} %get-tuple-element.6.refs_0_, bf16[512,256]{1,0:T(8,128)(2,1)S(1)} %get-tuple-element.7.refs_1_, bf16[512,256]{1,0:T(8,128)(2,1)S(1)} %get-tuple-element.8.refs_2_), custom_call_target="tpu_custom_call" | custom-call | tf_op jit(solution)/shard_map/pallas_call | solution.py:348
